TPU v7x, 32 devices: a whole 2x2x4 slice. The times are simulated.
32 devices in a mesh: dp: 8 (over z, x), fsdp: 4 (over y, core).
Axes of the slice: x: 2, y: 2, z: 4, core: 2. Of those that a mesh axis runs over, the one named last changes fastest.
Arguments:
- block_input: bfloat16 [18432, 768], P(('dp', 'fsdp')), may hold values from -6 to 6
- cotangent: bfloat16 [18432, 768], P(('dp', 'fsdp')), may hold values from -6 to 6
- time_embed: bfloat16 [32, 128], P(('dp', 'fsdp')), may hold values from -6 to 6
- ada_weight: bfloat16 [128, 4608], P('fsdp'), may hold values from -0.25 to 0.25
- ada_bias: bfloat16 [4608], P('fsdp'), may hold values from -2 to 2
- attn_gain: bfloat16 [768], P('fsdp'), may hold values from 0.5 to 1.5
- qkv_weight: bfloat16 [768, 2304], P('fsdp'), may hold values from -0.21875 to 0.21875
- out_weight: bfloat16 [768, 768], P('fsdp'), may hold values from -0.875 to 0.875
- mlp_gain: bfloat16 [768], P('fsdp'), may hold values from 0.5 to 1.5
- up_weight: bfloat16 [768, 3072], P('fsdp'), may hold values from -0.21875 to 0.21875
- up_bias: bfloat16 [3072], P('fsdp'), may hold values from -2 to 2
- down_weight: bfloat16 [3072, 768], P('fsdp'), may hold values from -0.109375 to 0.109375
- down_bias: bfloat16 [768], P('fsdp'), may hold values from -2 to 2
Outputs:
- block_output: bfloat16 [18432, 768], P(('dp', 'fsdp'))
- input_grad: float32 [18432, 768], P(('dp', 'fsdp'))
- time_grad: float32 [32, 128], P(('dp', 'fsdp'))
- ada_weight_grad: float32 [128, 4608], P('fsdp')
- ada_bias_grad: float32 [4608], P('fsdp')
- attn_gain_grad: float32 [768], P('fsdp')
- qkv_weight_grad: float32 [768, 2304], P('fsdp')
- out_weight_grad: float32 [768, 768], P('fsdp')
- mlp_gain_grad: float32 [768], P('fsdp')
- up_weight_grad: float32 [768, 3072], P('fsdp')
- up_bias_grad: float32 [3072], P('fsdp')
- down_weight_grad: float32 [3072, 768], P('fsdp')
- down_bias_grad: float32 [768], P('fsdp')
All inputs are finite; a program needn't handle non-finite values.
Results may differ from a plain program's by a relative error of at most 0.015.
The roundings to bfloat16 on the way count: a program that leaves them out, or rounds other values in their place, can miss the bound.
Values may be sent and summed in bfloat16 or wider, within the bound.
No kernel may reach another device: no remote copies, remote signals or barrier semaphores. Data moves between devices by JAX's collectives and lax.ppermute only.
A program may use at most 192 MiB of HBM per device.

v0:
```python
from functools import partial
import jax
import jax.numpy as jnp
from jax import lax
from jax.sharding import PartitionSpec as P

HEAD_DIM = 64


def norm_modulate(values, gain, shift, scale):
    centre = jnp.mean(values, axis=-1, keepdims=True)
    centred = values - centre
    spread = jnp.mean(centred * centred, axis=-1, keepdims=True)
    return centred * lax.rsqrt(spread + 1e-05) * gain * (1.0 + scale) + shift


def rotary_tables(length, head_dim):
    half_dim = head_dim // 2
    position = jnp.arange(length).astype(jnp.float32)[:, None]
    frequency = 10000.0 ** (-2.0 * jnp.arange(half_dim).astype(jnp.float32) / head_dim)
    angles = position * frequency[None, :]
    return (jnp.cos(angles), jnp.sin(angles))


def rotate(tensor, cosines, sines):
    half_dim = tensor.shape[-1] // 2
    first = tensor[..., :half_dim]
    second = tensor[..., half_dim:]
    cos_b = cosines[:, None, :]
    sin_b = sines[:, None, :]
    return jnp.concatenate(
        [first * cos_b - second * sin_b, second * cos_b + first * sin_b], axis=-1
    )


def unrotate(tensor, cosines, sines):
    half_dim = tensor.shape[-1] // 2
    first = tensor[..., :half_dim]
    second = tensor[..., half_dim:]
    cos_b = cosines[:, None, :]
    sin_b = sines[:, None, :]
    return jnp.concatenate(
        [first * cos_b + second * sin_b, second * cos_b - first * sin_b], axis=-1
    )


def head_scores(query_h, key_h):
    return jnp.dot(query_h, key_h.T, preferred_element_type=jnp.float32) * HEAD_DIM ** (-0.5)


def attend_head(triple):
    query_h, key_h, value_h = triple
    scores = head_scores(query_h, key_h)
    row_max = jnp.max(scores, axis=-1, keepdims=True)
    shifted = jnp.exp(scores - row_max)
    row_total = jnp.sum(shifted, axis=-1, keepdims=True)
    weights = (shifted / row_total).astype(jnp.bfloat16)
    return (
        jnp.dot(weights, value_h, preferred_element_type=jnp.float32),
        row_max[:, 0],
        row_total[:, 0],
    )


def head_grads(items):
    query_h, key_h, value_h, grad_h, row_max, row_total = items
    scores = head_scores(query_h, key_h)
    probs = jnp.exp(scores - row_max[:, None]) / row_total[:, None]
    probs_low = probs.astype(jnp.bfloat16)
    value_grad = jnp.dot(probs_low.T, grad_h, preferred_element_type=jnp.float32)
    prob_grad = jnp.dot(grad_h, value_h.T, preferred_element_type=jnp.float32)
    score_grad = (probs * (prob_grad - jnp.sum(probs * prob_grad, axis=-1, keepdims=True))).astype(
        jnp.bfloat16
    )
    query_grad = jnp.dot(score_grad, key_h, preferred_element_type=jnp.float32) * HEAD_DIM ** (-0.5)
    key_grad = jnp.dot(score_grad.T, query_h, preferred_element_type=jnp.float32) * HEAD_DIM ** (
        -0.5
    )
    return (query_grad, key_grad, value_grad)


def run_forward(block32, cond, attn_set, mlp_set, cosines, sines):
    ada_weight, ada_bias, attn_gain, qkv_weight, out_weight = attn_set
    mlp_gain, up_weight, up_bias, down_weight, down_bias = mlp_set
    length, width = block32.shape
    heads = width // HEAD_DIM
    modulation = jnp.dot(cond, ada_weight, preferred_element_type=jnp.float32) + ada_bias.astype(
        jnp.float32
    )
    pieces = [modulation[:, index * width : (index + 1) * width] for index in range(6)]
    attn_in = norm_modulate(block32, attn_gain.astype(jnp.float32), pieces[0], pieces[1]).astype(
        jnp.bfloat16
    )
    qkv_proj = jnp.dot(attn_in, qkv_weight, preferred_element_type=jnp.float32)
    queries = (
        rotate(qkv_proj[:, :width].reshape(length, heads, HEAD_DIM), cosines, sines)
        .astype(jnp.bfloat16)
        .transpose(1, 0, 2)
    )
    keys = (
        rotate(qkv_proj[:, width : 2 * width].reshape(length, heads, HEAD_DIM), cosines, sines)
        .astype(jnp.bfloat16)
        .transpose(1, 0, 2)
    )
    values = (
        qkv_proj[:, 2 * width :]
        .reshape(length, heads, HEAD_DIM)
        .astype(jnp.bfloat16)
        .transpose(1, 0, 2)
    )
    head_out, row_max, row_total = lax.map(attend_head, (queries, keys, values))
    attended = head_out.transpose(1, 0, 2).reshape(length, width).astype(jnp.bfloat16)
    attn_branch = jnp.dot(attended, out_weight, preferred_element_type=jnp.float32)
    middle = block32 + pieces[2] * attn_branch
    mlp_in = norm_modulate(middle, mlp_gain.astype(jnp.float32), pieces[3], pieces[4]).astype(
        jnp.bfloat16
    )
    pre_act = jnp.dot(mlp_in, up_weight, preferred_element_type=jnp.float32) + up_bias.astype(
        jnp.float32
    )
    activ = jax.nn.gelu(pre_act, approximate=True).astype(jnp.bfloat16)
    mlp_branch = jnp.dot(activ, down_weight, preferred_element_type=jnp.float32) + down_bias.astype(
        jnp.float32
    )
    output = (middle + pieces[5] * mlp_branch).astype(jnp.bfloat16)
    saved = (
        modulation,
        attn_in,
        queries,
        keys,
        values,
        row_max,
        row_total,
        attended,
        attn_branch,
        middle,
        mlp_in,
        pre_act,
        activ,
        mlp_branch,
    )
    return (output, saved)


def local(
    block_input,
    cotangent,
    time_embed,
    ada_weight,
    ada_bias,
    attn_gain,
    qkv_weight,
    out_weight,
    mlp_gain,
    up_weight,
    up_bias,
    down_weight,
    down_bias,
):
    length, width = block_input.shape
    heads = width // HEAD_DIM
    cosines, sines = rotary_tables(length, HEAD_DIM)
    block32 = block_input.astype(jnp.float32)

    def gather_attention():
        return (
            lax.all_gather(ada_weight, "fsdp", axis=0, tiled=True),
            lax.all_gather(ada_bias, "fsdp", axis=0, tiled=True),
            lax.all_gather(attn_gain, "fsdp", axis=0, tiled=True),
            lax.all_gather(qkv_weight, "fsdp", axis=0, tiled=True),
            lax.all_gather(out_weight, "fsdp", axis=0, tiled=True),
        )

    def gather_feed():
        return (
            lax.all_gather(mlp_gain, "fsdp", axis=0, tiled=True),
            lax.all_gather(up_weight, "fsdp", axis=0, tiled=True),
            lax.all_gather(up_bias, "fsdp", axis=0, tiled=True),
            lax.all_gather(down_weight, "fsdp", axis=0, tiled=True),
            lax.all_gather(down_bias, "fsdp", axis=0, tiled=True),
        )

    attn_full = gather_attention()
    mlp_full = gather_feed()
    block_output, saved = run_forward(block32, time_embed, attn_full, mlp_full, cosines, sines)
    attn_back = gather_attention()
    mlp_back = gather_feed()
    unused_output, saved_back = run_forward(
        block32, time_embed, attn_back, mlp_back, cosines, sines
    )
    (
        modulation,
        attn_in,
        queries,
        keys,
        values,
        row_max,
        row_total,
        attended,
        attn_branch,
        middle,
        mlp_in,
        pre_act,
        activ,
        mlp_branch,
    ) = saved_back
    ada_full, ada_bias_full, attn_gain_full, qkv_full, out_full = attn_back
    mlp_gain_full, up_full, up_bias_full, down_full, down_bias_full = mlp_back
    pieces = [modulation[:, index * width : (index + 1) * width] for index in range(6)]
    grad32 = cotangent.astype(jnp.float32)
    mlp_grad = (pieces[5] * grad32).astype(jnp.bfloat16)
    gate_m_grad = jnp.sum(grad32 * mlp_branch, axis=0, keepdims=True)
    down_weight_grad = jnp.dot(activ.T, mlp_grad, preferred_element_type=jnp.float32)
    down_bias_grad = jnp.sum(mlp_grad.astype(jnp.float32), axis=0)
    activ_grad = jnp.dot(mlp_grad, down_full.T, preferred_element_type=jnp.float32)
    unused_act, gelu_back = jax.vjp(partial(jax.nn.gelu, approximate=True), pre_act)
    pre_grad = gelu_back(activ_grad)[0].astype(jnp.bfloat16)
    up_weight_grad = jnp.dot(mlp_in.T, pre_grad, preferred_element_type=jnp.float32)
    up_bias_grad = jnp.sum(pre_grad.astype(jnp.float32), axis=0)
    mlp_in_grad = jnp.dot(pre_grad, up_full.T, preferred_element_type=jnp.float32)
    unused_norm, norm_back_m = jax.vjp(
        norm_modulate, middle, mlp_gain_full.astype(jnp.float32), pieces[3], pieces[4]
    )
    middle_part, mlp_gain_grad, shift_m_grad, scale_m_grad = norm_back_m(mlp_in_grad)
    middle_grad = grad32 + middle_part
    mlp_shares = (
        lax.psum_scatter(
            mlp_gain_grad.astype(jnp.bfloat16), "fsdp", scatter_dimension=0, tiled=True
        ).astype(jnp.float32),
        lax.psum_scatter(
            up_weight_grad.astype(jnp.bfloat16), "fsdp", scatter_dimension=0, tiled=True
        ).astype(jnp.float32),
        lax.psum_scatter(
            up_bias_grad.astype(jnp.bfloat16), "fsdp", scatter_dimension=0, tiled=True
        ).astype(jnp.float32),
        lax.psum_scatter(
            down_weight_grad.astype(jnp.bfloat16), "fsdp", scatter_dimension=0, tiled=True
        ).astype(jnp.float32),
        lax.psum_scatter(
            down_bias_grad.astype(jnp.bfloat16), "fsdp", scatter_dimension=0, tiled=True
        ).astype(jnp.float32),
    )
    attn_grad = (pieces[2] * middle_grad).astype(jnp.bfloat16)
    gate_a_grad = jnp.sum(middle_grad * attn_branch, axis=0, keepdims=True)
    out_weight_grad = jnp.dot(attended.T, attn_grad, preferred_element_type=jnp.float32)
    attended_grad = jnp.dot(attn_grad, out_full.T, preferred_element_type=jnp.float32).astype(
        jnp.bfloat16
    )
    grad_heads = attended_grad.reshape(length, heads, HEAD_DIM).transpose(1, 0, 2)
    query_grad, key_grad, value_grad = lax.map(
        head_grads, (queries, keys, values, grad_heads, row_max, row_total)
    )
    query_grad = unrotate(query_grad.transpose(1, 0, 2), cosines, sines).reshape(length, width)
    key_grad = unrotate(key_grad.transpose(1, 0, 2), cosines, sines).reshape(length, width)
    value_grad = value_grad.transpose(1, 0, 2).reshape(length, width)
    qkv_grad = jnp.concatenate([query_grad, key_grad, value_grad], axis=1).astype(jnp.bfloat16)
    qkv_weight_grad = jnp.dot(attn_in.T, qkv_grad, preferred_element_type=jnp.float32)
    attn_in_grad = jnp.dot(qkv_grad, qkv_full.T, preferred_element_type=jnp.float32)
    unused_first, norm_back_a = jax.vjp(
        norm_modulate, block32, attn_gain_full.astype(jnp.float32), pieces[0], pieces[1]
    )
    input_part, attn_gain_grad, shift_a_grad, scale_a_grad = norm_back_a(attn_in_grad)
    input_grad = middle_grad + input_part
    modulation_grad = jnp.concatenate(
        [shift_a_grad, scale_a_grad, gate_a_grad, shift_m_grad, scale_m_grad, gate_m_grad], axis=1
    ).astype(jnp.bfloat16)
    ada_weight_grad = jnp.dot(time_embed.T, modulation_grad, preferred_element_type=jnp.float32)
    ada_bias_grad = modulation_grad.astype(jnp.float32)[0]
    time_grad = jnp.dot(modulation_grad, ada_full.T, preferred_element_type=jnp.float32)
    attn_shares = (
        lax.psum_scatter(
            ada_weight_grad.astype(jnp.bfloat16), "fsdp", scatter_dimension=0, tiled=True
        ).astype(jnp.float32),
        lax.psum_scatter(
            ada_bias_grad.astype(jnp.bfloat16), "fsdp", scatter_dimension=0, tiled=True
        ).astype(jnp.float32),
        lax.psum_scatter(
            attn_gain_grad.astype(jnp.bfloat16), "fsdp", scatter_dimension=0, tiled=True
        ).astype(jnp.float32),
        lax.psum_scatter(
            qkv_weight_grad.astype(jnp.bfloat16), "fsdp", scatter_dimension=0, tiled=True
        ).astype(jnp.float32),
        lax.psum_scatter(
            out_weight_grad.astype(jnp.bfloat16), "fsdp", scatter_dimension=0, tiled=True
        ).astype(jnp.float32),
    )
    totals = lax.psum(
        (
            mlp_shares[0],
            mlp_shares[1],
            mlp_shares[2],
            mlp_shares[3],
            mlp_shares[4],
            attn_shares[0],
            attn_shares[1],
            attn_shares[2],
            attn_shares[3],
            attn_shares[4],
        ),
        "dp",
    )
    mlp_sums = totals[:5]
    attn_sums = totals[5:]
    return (
        block_output,
        input_grad,
        time_grad,
        attn_sums[0],
        attn_sums[1],
        attn_sums[2],
        attn_sums[3],
        attn_sums[4],
        mlp_sums[0],
        mlp_sums[1],
        mlp_sums[2],
        mlp_sums[3],
        mlp_sums[4],
    )


def solution(mesh):
    return jax.shard_map(
        local,
        mesh=mesh,
        in_specs=(
            P(("dp", "fsdp"), None),
            P(("dp", "fsdp"), None),
            P(("dp", "fsdp"), None),
            P("fsdp", None),
            P("fsdp"),
            P("fsdp"),
            P("fsdp", None),
            P("fsdp", None),
            P("fsdp"),
            P("fsdp", None),
            P("fsdp"),
            P("fsdp", None),
            P("fsdp"),
        ),
        out_specs=(
            P(("dp", "fsdp"), None),
            P(("dp", "fsdp"), None),
            P(("dp", "fsdp"), None),
            P("fsdp", None),
            P("fsdp"),
            P("fsdp"),
            P("fsdp", None),
            P("fsdp", None),
            P("fsdp"),
            P("fsdp", None),
            P("fsdp"),
            P("fsdp", None),
            P("fsdp"),
        ),
        check_vma=False,
    )
```

profile of v0, /device:TPU:0, one launch (start us, length us, event | category | flops | bytes accessed | tf_op | source)
XLA Modules:
  0.0 819.6 jit_solution(13222286501110139619)
XLA Ops:
  15.5 8.9 %all-reduce.10 = (bf16[768]{0:T(1024)(128)(2,1)S(1)}, bf16[768]{0:T(1024)(128)(2,1)S(1)}, bf16[768]{0:T(1024)(128)(2,1)S(1)}) all-reduce(bf16[768]{0:T(1024)(128)(2,1)S(1)} %dynamic-update-slice, bf16[768]{0:T(1024)(128)(2,1)S(1)} %dynamic-update-slice.2, bf16[768]{0:T(1024)(128)(2,1)S(1)} %dynamic-update-slice.1), channel_id=1, replica_groups=mesh['dp'=8,'fsdp'=4] {'fsdp'}, use_global_device_ids=true, to_apply=%add | all-reduce | flops 2304 | bytes 9216
  26.4 5.2 all-gather.1
  32.2 5.4 all-gather
  40.4 21.9 %all-gather.10.cloned.1.call-done = bf16[768,2304]{1,0:T(8,128)(2,1)} async-done(((bf16[192,2304]{1,0:T(8,128)(2,1)}), bf16[768,2304]{1,0:T(8,128)(2,1)}) %all-gather.10.cloned.1.call-update) | async-done | bytes 3538960 | tf_op jit(solution)/shard_map/all_gather | solution.py:170
  62.4 4.5 fusion.109
  67.0 2.0 fusion.117
  72.2 2.6 copy.57
  74.8 2.8 copy.52
  77.6 2.0 subtract_convert_fusion.2
  83.1 2.6 copy.56
  85.7 74.1 %while.42 = (s32[]{:T(128)}, bf16[12,576,64]{1,2,0:T(8,128)(2,1)}, f32[12,576]{1,0:T(8,128)}, f32[12,576]{1,0:T(8,128)}, bf16[12,576,64]{2,1,0:T(8,128)(2,1)S(1)...) while((s32[]{:T(128)}, bf16[12,576,64]{1,2,0:T(8,128)(2,1)}, ...), condition=%wide.region_11.12_spmd.clone, body=%wide.region_8.0_spmd.sunk.clone | while | flops 87255936 | bytes 4619613 | solution.py:111
  161.0 3.7 fusion.114
  165.7 7.6 fusion.112
  173.3 11.7 %fusion.121 = (bf16[3072]{0:T(1024)(128)(2,1)}, bf16[576,3072]{1,0:T(8,128)(2,1)S(1)}) fusion(f32[576,3072]{1,0:T(8,128)} %fusion.112, f32[3072]{0:T(1024)} %bitcast.202, bf16[3072,768]{1,0:T(8,128)(2,1)} %all-gather.16.cloned.1.call-done, bf16[576,768]{1,0:T(8,128)(2,1)S(1)} %copy-done.9, f32[768]{0:T(1024)} %get-tuple-element.214), kind=kOutput, calls=%fused_computation.198 | convolution fusion | flops 2758161408 | bytes 16241664 | tf_op jit(solution)/shard_map/dot_general | solution.py:215
  185.0 4.0 multiply_reduce_fusion.1
  191.2 2.3 convolution_convert_fusion.3
  193.4 3.7 convolution_convert_fusion.4
  197.1 2.3 copy.61
  199.4 113.5 %while.43 = (s32[]{:T(128)}, f32[12,576,64]{1,2,0:T(8,128)}, f32[12,576,64]{1,2,0:T(8,128)}, bf16[12,576,64]{1,2,0:T(8,128)(2,1)}, bf16[12,576,64]{2,1,0:T(8,128...) while((s32[]{:T(128)}, f32[12,576,64]{1,2,0:T(8,128)}, ...), condition=%wide.region_18.19_spmd.clone, body=%wide.region_16.18_spmd.sunk.clone | while | flops 215395776 | bytes 11369585 | solution.py:250
  313.0 2.8 add_convert_fusion.4
  317.4 2.8 fusion.78
  322.0 3.1 multiply_reduce_fusion.3
  329.3 9.4 %fusion.76 = bf16[768]{0:T(1024)(128)(2,1)} fusion(bf16[576,768]{1,0:T(8,128)(2,1)S(1)} %copy-done.9, bf16[3072,768]{1,0:T(8,128)(2,1)} %all-gather.16.cloned.1.call-done, f32[768]{0:T(1024)} %convert_element_type.257, f32[576,3072]{1,0:T(8,128)} %fusion.112, f32[3072]{0:T(1024)} %bitcast.203), kind=kOutput, calls=%fused_computation.110 | convolution fusion | flops 2737372416 | bytes 12698112 | tf_op jit(solution)/shard_map/dot_general | solution.py:122
  341.5 6.9 convolution_convert_fusion
  349.1 7.9 convolution_convert_fusion.2
  360.1 10.5 %convolution_convert_fusion.1 = bf16[3072,768]{1,0:T(8,128)(2,1)} fusion(bf16[576,768]{1,0:T(8,128)(2,1)S(1)} %copy-done.9, f32[768]{0:T(1024)S(1)} %copy-done.32, f32[576,3072]{1,0:T(8,128)} %fusion.112, f32[3072]{0:T(1024)S(1)} %bitcast.204), kind=kOutput, calls=%fused_computation.84 | convolution fusion | flops 2739290112 | bytes 12696576 | tf_op jit(solution)/shard_map/dot_general | solution.py:213
  371.8 35.5 %while.41 = (s32[]{:T(128)}, bf16[12,576,64]{1,2,0:T(8,128)(2,1)S(1)}, bf16[12,576,64]{2,1,0:T(8,128)(2,1)}, bf16[12,576,64]{2,1,0:T(8,128)(2,1)}, bf16[12,576,64]{2,1,0:T(8,128)(2,1)}) while((s32[]{:T(128)}, bf16[12,576,64]{1,2,0:T(8,128)(2,1)S(1)}, bf16[12,576,64]{2,1,0:T(8,128)(2,1)}, bf16[12,576,64]{2,1,0:T(8,128)(2,1)}, ...), condition=%wide.region_5.6_spmd.clone, body=%wide.region_2.5_spmd.sunk.clone | while | flops 87255936 | bytes 4752197 | solution.py:111
  409.9 11.0 %all-reduce.9 = (bf16[4608]{0:T(1024)(128)(2,1)S(1)}, bf16[768]{0:T(1024)(128)(2,1)S(1)}, bf16[768]{0:T(1024)(128)(2,1)S(1)}, bf16[3072]{0:T(1024)(128)(2,1)S(1)}, bf16[768]{0:T(1024)(128)(2,1)S(1)}) all-reduce(bf16[4608]{0:T(1024)(128)(2,1)S(1)} %dynamic-update-slice.8, ...), channel_id=3, replica_groups=mesh['dp'=8,'fsdp'=4] {'fsdp'}, use_global_device_ids=true, to_apply=%region_29.30.clone | all-reduce | flops 9984 | bytes 39936
  422.3 12.3 %add_convert_fusion.1 = bf16[576,768]{1,0:T(8,128)(2,1)} fusion(f32[576,768]{1,0:T(8,128)} %copy-done.10, bf16[3072,768]{1,0:T(8,128)(2,1)} %all-gather.16.cloned.1.call-done, bf16[768,3072]{1,0:T(8,128)(2,1)} %all-gather.14.cloned.1.call-done, f32[3072]{0:T(1024)S(1)} %bitcast.205, f32[768]{0:T(1024)S(1)} %copy-done.46, f32[768]{0:T(1024)S(1)} %copy-done.48, ...), kind=kOutput, calls=%fused_computation.122 | convolution fusion | flops 5457936384 | bytes 12123648 | tf_op jit(solution)/shard_map/dot_general | solution.py:122
  434.6 26.3 %reduce-scatter.12.cloned.1.call-done = bf16[192,3072]{1,0:T(8,128)(2,1)} async-done(((bf16[768,3072]{1,0:T(8,128)(2,1)}), bf16[192,3072]{1,0:T(8,128)(2,1)}) %reduce-scatter.12.cloned.1.call-update) | async-done | bytes 1179664 | tf_op jit(solution)/shard_map/reduce_scatter | solution.py:230
  460.9 50.4 %reduce-scatter.14.cloned.1.call-done = bf16[768,768]{1,0:T(8,128)(2,1)} async-done(((bf16[3072,768]{1,0:T(8,128)(2,1)}), bf16[768,768]{1,0:T(8,128)(2,1)}) %reduce-scatter.14.cloned.1.call-update) | async-done | bytes 1179664 | tf_op jit(solution)/shard_map/reduce_scatter | solution.py:236
  511.3 301.2 %all-reduce.12 = (f32[32,4608]{1,0:T(8,128)}, f32[1152]{0:T(1024)}, f32[192]{0:T(256)}, f32[192,2304]{1,0:T(8,128)}, f32[192,768]{1,0:T(8,128)}, /*index=5*/f32[...) all-reduce(bf16[32,4608]{1,0:T(8,128)(2,1)} %reduce-scatter.6.clone, ...), channel_id=1, replica_groups=mesh['dp'=8,'fsdp'=4] {'dp'}, use_global_device_ids=true, to_apply=%region_28.29 | all-reduce | flops 1919424 | bytes 11521536 | tf_op jit(solution)/shard_map/psum | solution.py:287
  (422 shorter events, 263.2 us)
Async XLA Ops:
  7.2 30.9 %all-gather.8.cloned.1.call-start = ((), (), s32[]{:S(2)}) async-start(), calls=%async_computation.5 | async-start | bytes 1474560 | tf_op jit(solution)/shard_map/all_gather | solution.py:167
  7.9 54.4 %all-gather.10.cloned.1.call-start = ((), (), s32[]{:S(2)}) async-start(), calls=%async_computation.6 | async-start | bytes 4423680 | tf_op jit(solution)/shard_map/all_gather | solution.py:170
  8.7 151.1 %all-gather.12.cloned.1.call-start = ((), (), s32[]{:S(2)}) async-start(), calls=%async_computation.7 | async-start | bytes 1474560 | tf_op jit(solution)/shard_map/all_gather | solution.py:171
  9.4 156.2 %all-gather.14.cloned.1.call-start = ((), (), s32[]{:S(2)}) async-start(), calls=%async_computation.8 | async-start | bytes 5898240 | tf_op jit(solution)/shard_map/all_gather | solution.py:177
  10.0 163.3 %all-gather.16.cloned.1.call-start = ((), (), s32[]{:S(2)}) async-start(), calls=%async_computation.9 | async-start | bytes 5898240 | tf_op jit(solution)/shard_map/all_gather | solution.py:179
  10.6 424.1 %reduce-scatter.10.cloned.1.call-start = ((), (), s32[]{:S(2)}) async-start(), calls=%async_computation.12 | async-start | bytes 1474560 | tf_op jit(solution)/shard_map/reduce_scatter | solution.py:283
  10.8 13.6 %copy-start.51 = (bf16[768]{0:T(1024)(128)(2,1)S(1)}, bf16[768]{0:T(1024)(128)(2,1)}, u32[]{:S(2)}) copy-start(bf16[768]{0:T(1024)(128)(2,1)} %param.29) | copy-start | bytes 4612
  10.9 14.9 %copy-start = (bf16[576,768]{1,0:T(8,128)(2,1)S(1)}, bf16[576,768]{1,0:T(8,128)(2,1)}, u32[]{:S(2)}) copy-start(bf16[576,768]{1,0:T(8,128)(2,1)} %param.19) | copy-start | bytes 2654212
  12.0 14.3 %copy-start.47 = (bf16[1152]{0:T(1024)(128)(2,1)S(1)}, bf16[1152]{0:T(1024)(128)(2,1)}, u32[]{:S(2)}) copy-start(bf16[1152]{0:T(1024)(128)(2,1)} %param.23) | copy-start | bytes 6916
  24.5 42.3 %copy-start.17 = (f32[768]{0:T(1024)}, f32[768]{0:T(1024)S(1)}, u32[]{:S(2)}) copy-start(f32[768]{0:T(1024)S(1)} %convert_element_type.245) | copy-start | bytes 9220
  26.3 40.5 %copy-start.23 = (f32[576]{0:T(1024)}, f32[576]{0:T(1024)S(1)}, u32[]{:S(2)}) copy-start(f32[576]{0:T(1024)S(1)} %fusion.77) | copy-start | bytes 6916
  26.4 40.5 %copy-start.19 = (f32[576]{0:T(1024)}, f32[576]{0:T(1024)S(1)}, u32[]{:S(2)}) copy-start(f32[576]{0:T(1024)S(1)} %fusion.97) | copy-start | bytes 6916
  38.0 39.6 %copy-start.15 = (f32[576,32]{0,1:T(8,128)}, f32[576,32]{0,1:T(8,128)S(1)}, u32[]{:S(2)}) copy-start(f32[576,32]{0,1:T(8,128)S(1)} %get-tuple-element.313) | copy-start | bytes 221188
  38.0 39.6 %copy-start.16 = (f32[576,32]{0,1:T(8,128)}, f32[576,32]{0,1:T(8,128)S(1)}, u32[]{:S(2)}) copy-start(f32[576,32]{0,1:T(8,128)S(1)} %get-tuple-element.314) | copy-start | bytes 221188
  40.4 26.4 %copy-start.21 = (f32[768]{0:T(1024)}, f32[768]{0:T(1024)S(1)}, u32[]{:S(2)}) copy-start(f32[768]{0:T(1024)S(1)} %get-tuple-element.218) | copy-start | bytes 9220
  40.4 26.4 %copy-start.49 = (f32[768]{0:T(1024)}, f32[768]{0:T(1024)S(1)}, u32[]{:S(2)}) copy-start(f32[768]{0:T(1024)S(1)} %get-tuple-element.217) | copy-start | bytes 9220
  40.4 120.5 %copy-start.33 = (f32[768]{0:T(1024)}, f32[768]{0:T(1024)S(1)}, u32[]{:S(2)}) copy-start(f32[768]{0:T(1024)S(1)} %get-tuple-element.219) | copy-start | bytes 9220
  173.3 11.7 %copy-start.28 = (f32[576]{0:T(1024)S(1)}, f32[576]{0:T(1024)}, u32[]{:S(2)}) copy-start(f32[576]{0:T(1024)} %copy-done.27) | copy-start | bytes 6916
  173.3 11.7 %copy-start.36 = (f32[768]{0:T(1024)S(1)}, f32[768]{0:T(1024)}, u32[]{:S(2)}) copy-start(f32[768]{0:T(1024)} %convert_element_type.253) | copy-start | bytes 9220
  173.3 11.7 %copy-start.38 = (f32[576]{0:T(1024)S(1)}, f32[576]{0:T(1024)}, u32[]{:S(2)}) copy-start(f32[576]{0:T(1024)} %fusion.98) | copy-start | bytes 6916
  312.9 121.7 %reduce-scatter.6.cloned.1.call-start = ((), (), s32[]{:S(2)}) async-start(), calls=%async_computation.10 | async-start | bytes 1474560 | tf_op jit(solution)/shard_map/reduce_scatter | solution.py:271
  341.5 93.2 %reduce-scatter.8.cloned.1.call-start = ((), (), s32[]{:S(2)}) async-start(), calls=%async_computation.11 | async-start | bytes 4423680 | tf_op jit(solution)/shard_map/reduce_scatter | solution.py:280
  348.5 112.4 %reduce-scatter.12.cloned.1.call-start = ((), (), s32[]{:S(2)}) async-start(), calls=%async_computation.13 | async-start | bytes 5898240 | tf_op jit(solution)/shard_map/reduce_scatter | solution.py:230
  357.1 154.2 %reduce-scatter.14.cloned.1.call-start = ((), (), s32[]{:S(2)}) async-start(), calls=%async_computation.14 | async-start | bytes 5898240 | tf_op jit(solution)/shard_map/reduce_scatter | solution.py:236
  371.8 35.5 %copy-start.11 = (bf16[768,768]{1,0:T(8,128)(2,1)S(1)}, bf16[768,768]{1,0:T(8,128)(2,1)}, u32[]{:S(2)}) copy-start(bf16[768,768]{1,0:T(8,128)(2,1)} %all-gather.12.cloned.1.call-done) | copy-start | bytes 3538948
  371.8 35.5 %copy-start.35 = (f32[768]{0:T(1024)S(1)}, f32[768]{0:T(1024)}, u32[]{:S(2)}) copy-start(f32[768]{0:T(1024)} %copy-done.33) | copy-start | bytes 9220
  408.4 13.0 %copy-start.7 = (bf16[128,4608]{1,0:T(8,128)(2,1)S(1)}, bf16[128,4608]{1,0:T(8,128)(2,1)}, u32[]{:S(2)}) copy-start(bf16[128,4608]{1,0:T(8,128)(2,1)} %all-gather.8.cloned.1.call-done) | copy-start | bytes 3538948
  408.4 13.9 %copy-start.37 = (f32[768]{0:T(1024)S(1)}, f32[768]{0:T(1024)}, u32[]{:S(2)}) copy-start(f32[768]{0:T(1024)} %convert_element_type.253) | copy-start | bytes 9220
  408.4 13.9 %copy-start.40 = (f32[768]{0:T(1024)S(1)}, f32[768]{0:T(1024)}, u32[]{:S(2)}) copy-start(f32[768]{0:T(1024)} %get-tuple-element.216) | copy-start | bytes 9220
  408.4 13.9 %copy-start.42 = (f32[4,1,768]{2,1,0:T(1,128)S(1)}, f32[4,1,768]{2,1,0:T(1,128)}, u32[]{:S(2)}) copy-start(f32[4,1,768]{2,1,0:T(1,128)} %convert_element_type.288) | copy-start | bytes 36868
  408.4 13.9 %copy-start.46 = (f32[768]{0:T(1024)S(1)}, f32[768]{0:T(1024)}, u32[]{:S(2)}) copy-start(f32[768]{0:T(1024)} %convert_element_type.257) | copy-start | bytes 9220
  408.4 13.9 %copy-start.48 = (f32[768]{0:T(1024)S(1)}, f32[768]{0:T(1024)}, u32[]{:S(2)}) copy-start(f32[768]{0:T(1024)} %get-tuple-element.215) | copy-start | bytes 9220
  (38 other events, 112.5 us)
Sparse Core Ops, SparseCore 0:
  9.5 20.2 all-gather.7
  31.4 30.9 all-gather.9
  63.9 17.3 all-gather.11
  82.8 37.4 all-gather.13
  121.6 37.4 all-gather.15
  313.0 25.5 reduce-scatter.9
  341.8 25.6 reduce-scatter.5
  370.0 40.3 reduce-scatter.7
  412.9 47.9 reduce-scatter.11
  463.3 47.9 reduce-scatter.13
where the time goes:
time: 827 us; the launch traced here: 820 us
  blocking collectives  332 us (40%)
  matrix products  264 us (32%)
  waiting for transfers between devices  102 us (12%)
  local copies, waits for them, and re-layouts  74.4 us (9%)
  other arithmetic  28.6 us (3%)
  between operations  17.8 us (2%)
    psum x1, blocking collectives, local(): lax.psum((mlp_shares[0], mlp_shares[1], mlp_shares[2], mlp_shares[3], mlp...  301 us
    reduce_scatter x1, waiting for transfers between devices, local(): lax.psum_scatter(down_weight_grad.astype(jnp.bfloat16), 'fsdp', scatter_d...  50.4 us
    dot_general x36, matrix products, head_scores(): jnp.dot(query_h, key_h.T, preferred_element_type=jnp.float32)  50.3 us
    dot_general x24, matrix products, attend_head(): jnp.dot(weights, value_h, preferred_element_type=jnp.float32)  38.9 us
    dynamic_update_slice x24, local copies, waits for them, and re-layouts, run_forward(): head_out, row_max, row_total = lax.map(attend_head, (queries, keys, values))  32.2 us
    reduce_scatter x1, waiting for transfers between devices, local(): lax.psum_scatter(up_weight_grad.astype(jnp.bfloat16), 'fsdp', scatter_dim...  26.3 us
    dot_general x12, matrix products, head_grads(): jnp.dot(score_grad.T, query_h, preferred_element_type=jnp.float32)  23.3 us
    dot_general x12, matrix products, head_grads(): jnp.dot(probs_low.T, grad_h, preferred_element_type=jnp.float32)  22.6 us
  transfers between devices with their start and end apart: 10, of which 3 were waited for; matrix products, arithmetic and copies ran while one was open for 27% of the time, Pallas kernels for 0%

commit v1 on v0

--- a/solution.py
+++ b/solution.py
@@ -1,10 +1,40 @@
+import functools
 from functools import partial
 import jax
 import jax.numpy as jnp
 from jax import lax
 from jax.sharding import PartitionSpec as P
+from jax.lax import axis_index, ppermute, psum
 
 HEAD_DIM = 64
+
+
+def match_words(vec, which_dim):
+    frame_out = list(vec.shape[1:])
+    frame_out[which_dim] *= vec.shape[0]
+    return jnp.moveaxis(vec, 0, which_dim).reshape(frame_out)
+
+
+def stages_all_step_on(x_in, mesh_name, pos_dim):
+    shares = psum(1, mesh_name)
+    sides = tuple(((i, (i + 1) % shares) for i in range(shares)))
+    line_up = tuple(((k, no) for no, k in sides))
+    k_now, odd = ([], [])
+    for q in [*range(shares - 1)]:
+        if q % 2 == 0:
+            t1 = ppermute(k_now[-1] if k_now else x_in, mesh_name, sides)
+            k_now.append(t1)
+        else:
+            odd.append(ppermute(odd[-1] if odd else x_in, mesh_name, line_up))
+    seen_now = jnp.stack([*k_now[::-1], x_in, *odd])
+    left_arr = len(k_now)
+    r1 = axis_index(mesh_name)
+    now = r1 - left_arr
+    seen_now = seen_now[(jnp.arange(shares) - now) % shares]
+    return match_words(seen_now, pos_dim)
+
+
+check_series_for = functools.partial(stages_all_step_on, mesh_name="fsdp", pos_dim=0)
 
 
 def norm_modulate(values, gain, shift, scale):
@@ -167,7 +197,7 @@
             lax.all_gather(ada_weight, "fsdp", axis=0, tiled=True),
             lax.all_gather(ada_bias, "fsdp", axis=0, tiled=True),
             lax.all_gather(attn_gain, "fsdp", axis=0, tiled=True),
-            lax.all_gather(qkv_weight, "fsdp", axis=0, tiled=True),
+            check_series_for(qkv_weight),
             lax.all_gather(out_weight, "fsdp", axis=0, tiled=True),
         )
 

time: 827 us -> 866 us (1.047)
  blocking collectives: 332 us -> 345 us
  local copies, waits for them, and re-layouts: 74.4 us -> 86.6 us
  other arithmetic: 28.6 us -> 39.5 us
    all_gather x1 -> x0, waiting for transfers between devices: 21.9 us -> none  [gather_attention(): lax.all_gather(qkv_weight, 'fsdp', axis=0, tiled=True)]
    ppermute x0 -> x3, waiting for transfers between devices: none -> 21.7 us  [the longest x2 21.7 us: stages_all_step_on(): t1 = ppermute(k_now[-1] if k_now else x_in, mesh_name, sides)]
    unnamed x2, blocking collectives: 20 us -> 33.5 us
    unnamed x136 -> x128, local copies, waits for them, and re-layouts: 14.6 us -> 20.6 us
  transfers between devices with their start and end apart: 10 -> 12, of which waited for: 3 -> 3; matrix products, arithmetic and copies ran while one was open for 27% -> 28% of each run, Pallas kernels for 0% -> 0%
where the time goes in v1:
time: 866 us; the launch traced here: 857 us
  blocking collectives  345 us (40%)
  matrix products  264 us (30%)
  waiting for transfers between devices  101 us (12%)
  local copies, waits for them, and re-layouts  86.6 us (10%)
  other arithmetic  39.5 us (5%)
  between operations  17.3 us (2%)
    psum x1, blocking collectives, local(): lax.psum((mlp_shares[0], mlp_shares[1], mlp_shares[2], mlp_shares[3], mlp...  301 us
    reduce_scatter x1, waiting for transfers between devices, local(): lax.psum_scatter(down_weight_grad.astype(jnp.bfloat16), 'fsdp', scatter_d...  50.5 us
    dot_general x36, matrix products, head_scores(): jnp.dot(query_h, key_h.T, preferred_element_type=jnp.float32)  50.3 us
    dot_general x24, matrix products, attend_head(): jnp.dot(weights, value_h, preferred_element_type=jnp.float32)  38.8 us
    unnamed x2, blocking collectives  33.5 us
    dynamic_update_slice x24, local copies, waits for them, and re-layouts, run_forward(): head_out, row_max, row_total = lax.map(attend_head, (queries, keys, values))  32.2 us
    reduce_scatter x1, waiting for transfers between devices, local(): lax.psum_scatter(up_weight_grad.astype(jnp.bfloat16), 'fsdp', scatter_dim...  26.4 us
    dot_general x12, matrix products, head_grads(): jnp.dot(score_grad.T, query_h, preferred_element_type=jnp.float32)  23.3 us
  transfers between devices with their start and end apart: 12, of which 3 were waited for; matrix products, arithmetic and copies ran while one was open for 28% of the time, Pallas kernels for 0%

profile of v1, /device:TPU:0, one launch (start us, length us, event | category | flops | bytes accessed | tf_op | source)
XLA Modules:
  0.0 857.5 jit_solution(10456538921583791587)
XLA Ops:
  19.8 22.7 %all-reduce.10 = (bf16[768]{0:T(1024)(128)(2,1)}, bf16[768]{0:T(1024)(128)(2,1)}, bf16[768]{0:T(1024)(128)(2,1)}) all-reduce(bf16[768]{0:T(1024)(128)(2,1)} %dynamic-update-slice, bf16[768]{0:T(1024)(128)(2,1)} %copy-done.47, bf16[768]{0:T(1024)(128)(2,1)S(1)} %dynamic-update-slice.1), channel_id=1, replica_groups=mesh['dp'=8,'fsdp'=4] {'fsdp'}, use_global_device_ids=true, to_apply=%add | all-reduce | flops 2304 | bytes 9216
  47.7 5.4 all-gather.1
  53.7 5.2 all-gather
  69.6 21.7 %collective-permute-done.1 = bf16[192,2304]{1,0:T(8,128)(2,1)} collective-permute-done((bf16[192,2304]{1,0:T(8,128)(2,1)S(1)}, bf16[192,2304]{1,0:T(8,128)(2,1)}, u32[]{:S(2)}, u32[]{:S(2)}) %collective-permute-start.1) | collective-permute-done | bytes 884768 | tf_op jit(solution)/shard_map/ppermute | solution.py:25
  91.3 3.2 pad_maximum_fusion
  94.5 4.7 gather_fusion
  99.3 4.5 fusion.111
  109.0 2.7 copy.57
  111.7 2.9 copy.52
  120.1 2.6 copy.56
  122.7 73.9 %while.42 = (s32[]{:T(128)}, bf16[12,576,64]{1,2,0:T(8,128)(2,1)}, f32[12,576]{1,0:T(8,128)}, f32[12,576]{1,0:T(8,128)}, bf16[12,576,64]{2,1,0:T(8,128)(2,1)S(1)...) while((s32[]{:T(128)}, bf16[12,576,64]{1,2,0:T(8,128)(2,1)}, ...), condition=%wide.region_11.12_spmd.clone, body=%wide.region_8.11_spmd.sunk.clone | while | flops 87255936 | bytes 4619613 | solution.py:141
  197.8 3.7 fusion.116
  202.5 7.6 fusion.114
  210.2 11.7 %fusion.123 = (bf16[3072]{0:T(1024)(128)(2,1)}, bf16[576,3072]{1,0:T(8,128)(2,1)S(1)}) fusion(f32[576,3072]{1,0:T(8,128)} %fusion.114, f32[3072]{0:T(1024)} %bitcast.214, bf16[3072,768]{1,0:T(8,128)(2,1)} %all-gather.13.cloned.1.call-done, bf16[576,768]{1,0:T(8,128)(2,1)S(1)} %copy-done.10, f32[768]{0:T(1024)} %get-tuple-element.214), kind=kOutput, calls=%fused_computation.207 | convolution fusion | flops 2758161408 | bytes 16241664 | tf_op jit(solution)/shard_map/dot_general | solution.py:245
  221.9 4.0 multiply_reduce_fusion.1
  228.0 2.3 convolution_convert_fusion.3
  230.3 3.7 convolution_convert_fusion.4
  236.2 113.5 %while.43 = (s32[]{:T(128)}, f32[12,576,64]{1,2,0:T(8,128)}, f32[12,576,64]{1,2,0:T(8,128)}, bf16[12,576,64]{1,2,0:T(8,128)(2,1)}, bf16[12,576,64]{2,1,0:T(8,128...) while((s32[]{:T(128)}, f32[12,576,64]{1,2,0:T(8,128)}, ...), condition=%wide.region_18.19_spmd.clone, body=%wide.region_16.18_spmd.sunk.clone | while | flops 215395776 | bytes 11369585 | solution.py:280
  349.8 2.8 add_convert_fusion.4
  352.9 2.4 copy-done.9
  355.3 2.8 fusion.78
  359.9 3.1 multiply_reduce_fusion.3
  367.2 9.4 %fusion.76 = bf16[768]{0:T(1024)(128)(2,1)} fusion(bf16[576,768]{1,0:T(8,128)(2,1)S(1)} %copy-done.10, bf16[3072,768]{1,0:T(8,128)(2,1)} %all-gather.13.cloned.1.call-done, f32[768]{0:T(1024)} %convert_element_type.257, f32[576,3072]{1,0:T(8,128)} %fusion.114, f32[3072]{0:T(1024)} %bitcast.215), kind=kOutput, calls=%fused_computation.112 | convolution fusion | flops 2737372416 | bytes 12698112 | tf_op jit(solution)/shard_map/dot_general | solution.py:152
  379.4 6.9 convolution_convert_fusion
  387.0 7.9 convolution_convert_fusion.2
  398.0 10.5 %convolution_convert_fusion.1 = bf16[3072,768]{1,0:T(8,128)(2,1)} fusion(bf16[576,768]{1,0:T(8,128)(2,1)S(1)} %copy-done.10, f32[768]{0:T(1024)S(1)} %copy-done.34, f32[576,3072]{1,0:T(8,128)} %fusion.114, f32[3072]{0:T(1024)S(1)} %bitcast.216), kind=kOutput, calls=%fused_computation.85 | convolution fusion | flops 2739290112 | bytes 12696576 | tf_op jit(solution)/shard_map/dot_general | solution.py:243
  409.7 35.6 %while.41 = (s32[]{:T(128)}, bf16[12,576,64]{1,2,0:T(8,128)(2,1)S(1)}, bf16[12,576,64]{2,1,0:T(8,128)(2,1)}, bf16[12,576,64]{2,1,0:T(8,128)(2,1)}, bf16[12,576,64]{2,1,0:T(8,128)(2,1)}) while((s32[]{:T(128)}, bf16[12,576,64]{1,2,0:T(8,128)(2,1)S(1)}, bf16[12,576,64]{2,1,0:T(8,128)(2,1)}, bf16[12,576,64]{2,1,0:T(8,128)(2,1)}, ...), condition=%wide.region_5.6_spmd.clone, body=%wide.region_2.5_spmd.sunk.clone | while | flops 87255936 | bytes 4752197 | solution.py:141
  447.9 10.8 %all-reduce.9 = (bf16[4608]{0:T(1024)(128)(2,1)S(1)}, bf16[768]{0:T(1024)(128)(2,1)S(1)}, bf16[768]{0:T(1024)(128)(2,1)S(1)}, bf16[3072]{0:T(1024)(128)(2,1)S(1)}, bf16[768]{0:T(1024)(128)(2,1)S(1)}) all-reduce(bf16[4608]{0:T(1024)(128)(2,1)S(1)} %dynamic-update-slice.8, ...), channel_id=3, replica_groups=mesh['dp'=8,'fsdp'=4] {'fsdp'}, use_global_device_ids=true, to_apply=%region_29.30.clone | all-reduce | flops 9984 | bytes 39936
  460.1 12.4 %add_convert_fusion.1 = bf16[576,768]{1,0:T(8,128)(2,1)} fusion(f32[576,768]{1,0:T(8,128)} %copy-done.11, bf16[3072,768]{1,0:T(8,128)(2,1)} %all-gather.13.cloned.1.call-done, bf16[768,3072]{1,0:T(8,128)(2,1)} %all-gather.11.cloned.1.call-done, f32[3072]{0:T(1024)S(1)} %bitcast.217, f32[768]{0:T(1024)S(1)} %copy-done.49, f32[768]{0:T(1024)S(1)} %copy-done.50, ...), kind=kOutput, calls=%fused_computation.124 | convolution fusion | flops 5457936384 | bytes 12123648 | tf_op jit(solution)/shard_map/dot_general | solution.py:152
  472.5 26.4 %reduce-scatter.12.cloned.1.call-done = bf16[192,3072]{1,0:T(8,128)(2,1)} async-done(((bf16[768,3072]{1,0:T(8,128)(2,1)}), bf16[192,3072]{1,0:T(8,128)(2,1)}) %reduce-scatter.12.cloned.1.call-update) | async-done | bytes 1179664 | tf_op jit(solution)/shard_map/reduce_scatter | solution.py:260
  499.0 50.5 %reduce-scatter.14.cloned.1.call-done = bf16[768,768]{1,0:T(8,128)(2,1)} async-done(((bf16[3072,768]{1,0:T(8,128)(2,1)}), bf16[768,768]{1,0:T(8,128)(2,1)}) %reduce-scatter.14.cloned.1.call-update) | async-done | bytes 1179664 | tf_op jit(solution)/shard_map/reduce_scatter | solution.py:266
  549.5 301.2 %all-reduce.12 = (f32[32,4608]{1,0:T(8,128)}, f32[1152]{0:T(1024)}, f32[192]{0:T(256)}, f32[192,2304]{1,0:T(8,128)}, f32[192,768]{1,0:T(8,128)}, /*index=5*/f32[...) all-reduce(bf16[32,4608]{1,0:T(8,128)(2,1)} %reduce-scatter.6.clone, ...), channel_id=1, replica_groups=mesh['dp'=8,'fsdp'=4] {'dp'}, use_global_device_ids=true, to_apply=%region_28.29 | all-reduce | flops 1919424 | bytes 11521536 | tf_op jit(solution)/shard_map/psum | solution.py:317
  (421 shorter events, 283.8 us)
Async XLA Ops:
  7.2 59.4 %all-gather.7.cloned.1.call-start = ((), (), s32[]{:S(2)}) async-start(), calls=%async_computation.5 | async-start | bytes 1474560 | tf_op jit(solution)/shard_map/all_gather | solution.py:197
  7.9 188.7 %all-gather.9.cloned.1.call-start = ((), (), s32[]{:S(2)}) async-start(), calls=%async_computation.6 | async-start | bytes 1474560 | tf_op jit(solution)/shard_map/all_gather | solution.py:201
  8.7 193.8 %all-gather.11.cloned.1.call-start = ((), (), s32[]{:S(2)}) async-start(), calls=%async_computation.7 | async-start | bytes 5898240 | tf_op jit(solution)/shard_map/all_gather | solution.py:207
  9.4 200.7 %all-gather.13.cloned.1.call-start = ((), (), s32[]{:S(2)}) async-start(), calls=%async_computation.8 | async-start | bytes 5898240 | tf_op jit(solution)/shard_map/all_gather | solution.py:209
  9.5 53.5 %collective-permute-start = (bf16[192,2304]{1,0:T(8,128)(2,1)S(1)}, bf16[192,2304]{1,0:T(8,128)(2,1)S(1)}, u32[]{:S(2)}, u32[]{:S(2)}) collective-permute-start(bf16[192,2304]{1,0:T(8,128)(2,1)S(1)} %copy-done.16), channel_id=1, source_target_pairs={{0,1},{1,2},{2,3},{3,0},{4,5},{5,6},{6,7},{7,4},{8,9},{9,10},{10,1... | collective-permute-start | bytes 2654216 | tf_op jit(solution)/shard_map/ppermute | solution.py:25
  10.0 59.6 %collective-permute-start.2 = (bf16[192,2304]{1,0:T(8,128)(2,1)S(1)}, bf16[192,2304]{1,0:T(8,128)(2,1)S(1)}, u32[]{:S(2)}, u32[]{:S(2)}) collective-permute-start(bf16[192,2304]{1,0:T(8,128)(2,1)S(1)} %copy-done.16), channel_id=1, source_target_pairs={{1,0},{2,1},{3,2},{0,3},{5,4},{6,5},{7,6},{4,7},{9,8},{10,9},{11,1... | collective-permute-start | bytes 2654216 | tf_op jit(solution)/shard_map/ppermute | solution.py:28
  12.0 460.5 %reduce-scatter.10.cloned.1.call-start = ((), (), s32[]{:S(2)}) async-start(), calls=%async_computation.11 | async-start | bytes 1474560 | tf_op jit(solution)/shard_map/reduce_scatter | solution.py:313
  12.8 48.8 %copy-start = (bf16[576,768]{1,0:T(8,128)(2,1)S(1)}, bf16[576,768]{1,0:T(8,128)(2,1)}, u32[]{:S(2)}) copy-start(bf16[576,768]{1,0:T(8,128)(2,1)} %param.19) | copy-start | bytes 2654212
  63.0 28.4 %collective-permute-start.1 = (bf16[192,2304]{1,0:T(8,128)(2,1)S(1)}, bf16[192,2304]{1,0:T(8,128)(2,1)}, u32[]{:S(2)}, u32[]{:S(2)}) collective-permute-start(bf16[192,2304]{1,0:T(8,128)(2,1)S(1)} %collective-permute-done), channel_id=1, source_target_pairs={{0,1},{1,2},{2,3},{3,0},{4,5},{5,6},{6,7},{7,4},{8,9},{9,10},{10,1... | collective-permute-start | bytes 2654216 | tf_op jit(solution)/shard_map/ppermute | solution.py:25
  94.5 4.7 copy-start.23
  94.5 4.7 copy-start.51
  122.7 75.1 %copy-start.35 = (f32[768]{0:T(1024)S(1)}, f32[768]{0:T(1024)}, u32[]{:S(2)}) copy-start(f32[768]{0:T(1024)} %get-tuple-element.219) | copy-start | bytes 9220
  202.5 7.6 copy-start.10
  210.1 11.7 %copy-start.30 = (f32[576]{0:T(1024)S(1)}, f32[576]{0:T(1024)}, u32[]{:S(2)}) copy-start(f32[576]{0:T(1024)} %copy-done.29) | copy-start | bytes 6916
  210.1 11.7 %copy-start.38 = (f32[768]{0:T(1024)S(1)}, f32[768]{0:T(1024)}, u32[]{:S(2)}) copy-start(f32[768]{0:T(1024)} %convert_element_type.253) | copy-start | bytes 9220
  210.1 11.7 %copy-start.40 = (f32[576]{0:T(1024)S(1)}, f32[576]{0:T(1024)}, u32[]{:S(2)}) copy-start(f32[576]{0:T(1024)} %fusion.98) | copy-start | bytes 6916
  210.1 11.7 %copy-start.41 = (f32[768]{0:T(1024)S(1)}, f32[768]{0:T(1024)}, u32[]{:S(2)}) copy-start(f32[768]{0:T(1024)} %get-tuple-element.216) | copy-start | bytes 9220
  210.2 11.7 %copy-start.54 = (bf16[768,3072]{1,0:T(8,128)(2,1)S(1)}, bf16[768,3072]{1,0:T(8,128)(2,1)}, u32[]{:S(2)}) copy-start(bf16[768,3072]{1,0:T(8,128)(2,1)} %all-gather.11.cloned.1.call-done) | copy-start | bytes 14155780
  349.7 122.8 %reduce-scatter.6.cloned.1.call-start = ((), (), s32[]{:S(2)}) async-start(), calls=%async_computation.9 | async-start | bytes 1474560 | tf_op jit(solution)/shard_map/reduce_scatter | solution.py:301
  352.7 5.3 copy-start.14
  352.9 5.2 copy-start.15
  379.4 93.2 %reduce-scatter.8.cloned.1.call-start = ((), (), s32[]{:S(2)}) async-start(), calls=%async_computation.10 | async-start | bytes 4423680 | tf_op jit(solution)/shard_map/reduce_scatter | solution.py:310
  386.4 112.6 %reduce-scatter.12.cloned.1.call-start = ((), (), s32[]{:S(2)}) async-start(), calls=%async_computation.12 | async-start | bytes 5898240 | tf_op jit(solution)/shard_map/reduce_scatter | solution.py:260
  395.0 154.5 %reduce-scatter.14.cloned.1.call-start = ((), (), s32[]{:S(2)}) async-start(), calls=%async_computation.13 | async-start | bytes 5898240 | tf_op jit(solution)/shard_map/reduce_scatter | solution.py:266
  409.7 35.6 %copy-start.12 = (bf16[768,768]{1,0:T(8,128)(2,1)S(1)}, bf16[768,768]{1,0:T(8,128)(2,1)}, u32[]{:S(2)}) copy-start(bf16[768,768]{1,0:T(8,128)(2,1)} %all-gather.9.cloned.1.call-done) | copy-start | bytes 3538948
  409.7 35.6 %copy-start.37 = (f32[768]{0:T(1024)S(1)}, f32[768]{0:T(1024)}, u32[]{:S(2)}) copy-start(f32[768]{0:T(1024)} %get-tuple-element.219) | copy-start | bytes 9220
  446.4 12.7 %copy-start.7 = (bf16[128,4608]{1,0:T(8,128)(2,1)S(1)}, bf16[128,4608]{1,0:T(8,128)(2,1)}, u32[]{:S(2)}) copy-start(bf16[128,4608]{1,0:T(8,128)(2,1)} %all-gather.7.cloned.1.call-done) | copy-start | bytes 3538948
  446.4 13.7 %copy-start.39 = (f32[768]{0:T(1024)S(1)}, f32[768]{0:T(1024)}, u32[]{:S(2)}) copy-start(f32[768]{0:T(1024)} %convert_element_type.253) | copy-start | bytes 9220
  446.4 13.7 %copy-start.42 = (f32[768]{0:T(1024)S(1)}, f32[768]{0:T(1024)}, u32[]{:S(2)}) copy-start(f32[768]{0:T(1024)} %get-tuple-element.216) | copy-start | bytes 9220
  446.4 13.7 %copy-start.44 = (f32[4,1,768]{2,1,0:T(1,128)S(1)}, f32[4,1,768]{2,1,0:T(1,128)}, u32[]{:S(2)}) copy-start(f32[4,1,768]{2,1,0:T(1,128)} %convert_element_type.288) | copy-start | bytes 36868
  446.4 13.6 %copy-start.49 = (f32[768]{0:T(1024)S(1)}, f32[768]{0:T(1024)}, u32[]{:S(2)}) copy-start(f32[768]{0:T(1024)} %convert_element_type.257) | copy-start | bytes 9220
  446.4 13.6 %copy-start.50 = (f32[768]{0:T(1024)S(1)}, f32[768]{0:T(1024)}, u32[]{:S(2)}) copy-start(f32[768]{0:T(1024)} %get-tuple-element.215) | copy-start | bytes 9220
  (36 other events, 79.5 us)
Sparse Core Ops, SparseCore 0:
  9.6 26.6 all-gather.6
  37.8 17.5 all-gather.8
  56.9 45.3 all-gather.10
  103.8 37.5 all-gather.12
  349.9 25.8 reduce-scatter.9
  379.5 25.9 reduce-scatter.5
  408.0 40.3 reduce-scatter.7
  451.0 47.9 reduce-scatter.11
  501.5 47.9 reduce-scatter.13
